TPU v7x, 32 devices: a whole 2x2x4 slice. The times are simulated.
32 devices in a mesh: replica: 2 (over y), tp: 4 (over x, core), dp: 4 (over z).
Axes of the slice: x: 2, y: 2, z: 4, core: 2. Of those that a mesh axis runs over, the one named last changes fastest.
Arguments:
- tokens: bfloat16 [8192, 8192], P(('replica', 'dp'), 'tp'), parts along dimension 0, may hold values from -6 to 6
- query_weight: bfloat16 [8192, 4096], P(None, 'tp'), may hold values from -0.0625 to 0.0625
- value_weight: bfloat16 [8192, 1024], P(None, 'tp'), may hold values from -0.0625 to 0.0625
- adapter_down_factors: bfloat16 [256, 8192, 128], P('dp', 'tp'), may hold values from -0.0625 to 0.0625
- query_up_factors: bfloat16 [256, 64, 4096], P('dp', None, 'tp'), may hold values from -0.75 to 0.75
- value_up_factors: bfloat16 [256, 64, 1024], P('dp', None, 'tp'), may hold values from -0.75 to 0.75
- request_adapter: int32 [32], P('replica'), parts along dimension 0, may hold values from 0 to 255
- lengths: int32 [32], P('replica'), parts along dimension 0, may hold values from 1 to 1024, 4096 in all
- home: int32 [256], replicated, may hold values from 0 to 255, each once
Outputs:
- query: bfloat16 [8192, 4096], P(('replica', 'dp'), 'tp'), parts along dimension 0
- value: bfloat16 [8192, 1024], P(('replica', 'dp'), 'tp'), parts along dimension 0
There are 2 independent parts, one for each index of `replica`. A program takes and returns all parts, laid end to end along the dimension named above; an argument that names none is the same for every part. Nothing has to cross between parts.
Inputs may be any that keep to these rules, and one draw needn't show every extreme that they name: The lengths sum to 4096; the requests lie one after another in the token order. `home`: each of 0 to 255 appears once.
All inputs are finite; a program needn't handle non-finite values.
Results may differ from a plain program's by a relative error of at most 0.0031.
Values may be sent and summed in bfloat16 or wider, within the bound.
No kernel may reach another device: no remote copies, remote signals or barrier semaphores. Data moves between devices by JAX's collectives and lax.ppermute only.
A program may use at most 192 MiB of HBM per device.

v0:
```python
import jax
import jax.numpy as jnp
from jax import lax
from jax.sharding import PartitionSpec as P

adapter_scale = 0.5


def owners(lengths, first_row, count):
    starts = jnp.cumsum(lengths, dtype=jnp.int32) - lengths
    rows_here = first_row + jnp.arange(count, dtype=jnp.int32)
    return (
        jnp.sum((rows_here[:, None] >= starts[None, :]).astype(jnp.int32), axis=1, dtype=jnp.int32)
        - 1
    )


def body(
    tokens,
    query_weight,
    value_weight,
    adapter_down_factors,
    query_up_factors,
    value_up_factors,
    request_adapter,
    lengths,
    home,
):
    tok_rows = tokens.shape[0]
    stored_adapters = adapter_down_factors.shape[0]
    rank_extent = query_up_factors.shape[1]
    dp_index = lax.axis_index("dp")
    adapter_slots = home[request_adapter]
    holder = adapter_slots // stored_adapters
    location = adapter_slots % stored_adapters
    mine = holder == dp_index

    def select_rows(table):
        taken = jnp.take(table, location, axis=0)
        return jnp.where(mine[:, None, None], taken, jnp.zeros_like(taken))

    summed = (
        lax.psum(select_rows(adapter_down_factors), "dp").astype(jnp.float32),
        lax.psum(select_rows(query_up_factors), "dp").astype(jnp.float32),
        lax.psum(select_rows(value_up_factors), "dp").astype(jnp.float32),
    )
    down_f = summed[0].astype(jnp.bfloat16)
    up_q = summed[1].astype(jnp.bfloat16)
    up_v = summed[2].astype(jnp.bfloat16)
    owner = owners(lengths, dp_index * tok_rows, tok_rows)
    first_req = owner[0]
    last_req = owner[tok_rows - 1] + 1
    zero_q = jnp.zeros((tok_rows, query_weight.shape[1]), jnp.float32)
    zero_v = jnp.zeros((tok_rows, value_weight.shape[1]), jnp.float32)
    piece = lax.all_gather(tokens, "tp", axis=1, tiled=True)
    query_plain = jnp.dot(piece, query_weight, preferred_element_type=jnp.float32)
    value_plain = jnp.dot(piece, value_weight, preferred_element_type=jnp.float32)

    def down_group(request_number, total):
        factor = lax.dynamic_index_in_dim(down_f, request_number, 0, keepdims=False)
        product = jnp.dot(tokens, factor, preferred_element_type=jnp.float32)
        return total + jnp.where((owner == request_number)[:, None], product, 0.0)

    selected = lax.fori_loop(
        first_req, last_req, down_group, jnp.zeros((tok_rows, down_f.shape[2]), jnp.float32)
    )
    down = lax.psum(selected, "tp").astype(jnp.bfloat16)
    down_q = down[:, :rank_extent]
    down_v = down[:, rank_extent:]

    def up_group(request_number, totals):
        factor_q = lax.dynamic_index_in_dim(up_q, request_number, 0, keepdims=False)
        factor_v = lax.dynamic_index_in_dim(up_v, request_number, 0, keepdims=False)
        inside = (owner == request_number)[:, None]
        part_q = jnp.dot(down_q, factor_q, preferred_element_type=jnp.float32)
        part_v = jnp.dot(down_v, factor_v, preferred_element_type=jnp.float32)
        return (
            totals[0] + jnp.where(inside, part_q, 0.0),
            totals[1] + jnp.where(inside, part_v, 0.0),
        )

    query_lowrank, value_lowrank = lax.fori_loop(first_req, last_req, up_group, (zero_q, zero_v))
    query = (query_plain + adapter_scale * query_lowrank).astype(jnp.bfloat16)
    value = (value_plain + adapter_scale * value_lowrank).astype(jnp.bfloat16)
    return (query, value)


def solution(mesh):
    in_specs = (
        P(("replica", "dp"), "tp"),
        P(None, "tp"),
        P(None, "tp"),
        P("dp", "tp", None),
        P("dp", None, "tp"),
        P("dp", None, "tp"),
        P("replica"),
        P("replica"),
        P(),
    )
    out_specs = (P(("replica", "dp"), "tp"), P(("replica", "dp"), "tp"))
    return jax.shard_map(body, mesh=mesh, in_specs=in_specs, out_specs=out_specs, check_vma=False)
```

profile of v0, /device:TPU:20, one launch (start us, length us, event | category | flops | bytes accessed | tf_op | source)
XLA Modules:
  0.0 585.5 jit_solution(7345490909103174528)
XLA Ops:
  8.9 1.3 gather_fusion
  10.3 7.3 %gather_fusion.2 = bf16[16,2048,128]{2,1,0:T(8,128)(2,1)} fusion(bf16[64,2048,128]{2,1,0:T(8,128)(2,1)} %param.16, s32[1024]{0:T(1024)S(1)} %pad_clamp_fusion), kind=kCustom, calls=%fused_computation.2 | custom fusion | bytes 16777280 | tf_op jit(solution)/shard_map/jit(_take)/gather | solution.py:39
  17.6 5.4 gather_fusion.1
  22.9 7.7 %select_select_fusion = bf16[16,2048,128]{2,1,0:T(8,128)(2,1)} fusion(bf16[16,2048,128]{2,1,0:T(8,128)(2,1)} %gather_fusion.2, pred[16]{0:T(512)(128)(4,1)S(1)} %get-tuple-element.125, pred[16]{0:T(512)(128)(4,1)S(1)} %get-tuple-element.124), kind=kLoop, calls=%fused_computation.22 | loop fusion | flops 8388608 | bytes 16777248 | tf_op jit(solution)/shard_map/jit(_where)/select_n | solution.py:40
  30.7 1.6 select_select_fusion.1
  36.6 372.7 %all-reduce.4.cloned.1.call-done = (bf16[16,64,1024]{2,1,0:T(8,128)(2,1)}, bf16[16,2048,128]{2,1,0:T(8,128)(2,1)}, bf16[16,64,256]{2,1,0:T(8,128)(2,1)}) async-done(((bf16[16,64,1024]{2,1,0:T(8,128)(2,1)}, bf16[16,2048,128]{2,1,0:T(8,128)(2,1)}, bf16[16,64,256]{2,1,0:T(8,128)(2,1)}), (bf16[16,64,1024]{2,1,0:T(8,128)(2,1)}, bf16[16,2048,128]{2,1,0:T(8,128)(2,1)}, ...) | async-done | bytes 11010064 | tf_op jit(solution)/shard_map/psum | solution.py:44
  409.4 31.9 %while.22 = (s32[]{:T(128)}, f32[1024,128]{0,1:T(8,128)S(1)}, s32[]{:T(128)}, s32[1024]{0:T(1024)S(1)}, bf16[16,2048,128]{2,1,0:T(8,128)(2,1)}, /*index=5*/bf16[...) while((s32[]{:T(128)}, f32[1024,128]{0,1:T(8,128)S(1)}, s32[]{:T(128)}, s32[1024]{0:T(1024)S(1)}, ...), condition=%wide.region_6.7_spmd, body=%wide.region_5.6_spmd.sunk | while | flops 537134080 | bytes 5773447 | solution.py:64
  409.5 3.9 fusion.36
  413.5 3.9 fusion.36
  417.4 3.9 fusion.36
  421.4 3.9 fusion.36
  425.4 3.9 fusion.36
  429.4 3.9 fusion.36
  433.4 3.9 fusion.36
  437.4 3.9 fusion.36
  441.6 16.9 %all-reduce.5 = bf16[1024,128]{1,0:T(8,128)(2,1)S(1)} all-reduce(f32[1024,128]{1,0:T(8,128)S(1)} %copy.20), channel_id=1, replica_groups=mesh['replica'=2,'tp'=4,'dp'=4] {'tp'}, use_global_device_ids=true, to_apply=%region_7.8 | all-reduce | flops 131072 | bytes 786432 | tf_op jit(solution)/shard_map/psum | solution.py:67
  458.6 2.5 broadcast_in_dim.118
  461.2 81.0 %while.23 = (s32[]{:T(128)}, f32[1024,1024]{0,1:T(8,128)}, f32[1024,256]{0,1:T(8,128)S(1)}, s32[]{:T(128)}, s32[1024]{0:T(1024)S(1)}, /*index=5*/bf16[16,64,1024...) while((s32[]{:T(128)}, f32[1024,1024]{0,1:T(8,128)}, ...), condition=%wide.region_9.10_spmd, body=%wide.region_8.9_spmd.sunk | while | flops 170394624 | bytes 10919075 | solution.py:82
  464.0 5.0 bitcast_add_fusion.2
  474.1 5.0 bitcast_add_fusion.2
  479.0 1.1 fusion.41
  484.1 5.0 bitcast_add_fusion.2
  489.1 1.1 fusion.41
  494.1 5.0 bitcast_add_fusion.2
  504.2 5.0 bitcast_add_fusion.2
  514.2 5.0 bitcast_add_fusion.2
  519.2 1.1 fusion.41
  524.2 5.0 bitcast_add_fusion.2
  534.3 5.0 bitcast_add_fusion.2
  542.2 5.4 copy.21
  547.9 24.8 %add_convert_fusion = bf16[1024,1024]{1,0:T(8,128)(2,1)} fusion(f32[1024,1024]{1,0:T(8,128)} %copy.21, bf16[1024,8192]{1,0:T(8,128)(2,1)} %all-gather.2.cloned.1.call-done, bf16[8192,1024]{1,0:T(8,128)(2,1)} %param.14), kind=kOutput, calls=%fused_computation.23 | convolution fusion | flops 17183014912 | bytes 39845888 | tf_op jit(solution)/shard_map/dot_general | solution.py:56
  572.8 5.3 fusion.13
  (58 shorter events, 14.9 us)
Async XLA Ops:
  8.0 24.3 %copy-start = (bf16[64,64,256]{2,1,0:T(8,128)(2,1)S(1)}, bf16[64,64,256]{2,1,0:T(8,128)(2,1)}, u32[]{:S(2)}) copy-start(bf16[64,64,256]{2,1,0:T(8,128)(2,1)} %param.18) | copy-start | bytes 6291460
  8.0 401.4 %all-reduce.4.cloned.1.call-start = ((), (), s32[]{:S(2)}) async-start(), calls=%async_computation.1 | async-start | bytes 22020096 | tf_op jit(solution)/shard_map/psum | solution.py:44
  22.9 7.7 %copy-start.2 = (bf16[16,64,1024]{2,1,0:T(8,128)(2,1)S(1)}, bf16[16,64,1024]{2,1,0:T(8,128)(2,1)}, u32[]{:S(2)}) copy-start(bf16[16,64,1024]{2,1,0:T(8,128)(2,1)} %gather_fusion.1) | copy-start | bytes 6291460
  33.8 0.7 copy-start.3
  33.8 514.0 %all-gather.2.cloned.1.call-start = ((), (), s32[]{:S(2)}) async-start(), calls=%async_computation | async-start | bytes 20971520 | tf_op jit(solution)/shard_map/all_gather | solution.py:55
  547.9 24.9 %copy-start.4 = (bf16[1024,8192]{1,0:T(8,128)(2,1)S(1)}, bf16[1024,8192]{1,0:T(8,128)(2,1)}, u32[]{:S(2)}) copy-start(bf16[1024,8192]{1,0:T(8,128)(2,1)} %all-gather.2.cloned.1.call-done) | copy-start | bytes 50331652
  547.9 24.8 %copy-start.5 = (bf16[8192,256]{1,0:T(8,128)(2,1)S(1)}, bf16[8192,256]{1,0:T(8,128)(2,1)}, u32[]{:S(2)}) copy-start(bf16[8192,256]{1,0:T(8,128)(2,1)} %param.15) | copy-start | bytes 12582916
  572.8 5.3 copy-start.1
Sparse Core Ops, SparseCore 0:
  34.0 375.3 all-reduce.3
Sparse Core Ops, SparseCore 1:
  35.9 106.8 all-gather.1
where the time goes:
time: 587 us; the launch traced here: 585 us
  waiting for transfers between devices  373 us (64%)
  matrix products  110 us (19%)
  loops' own time  28.3 us (5%)
  local copies, waits for them, and re-layouts  24 us (4%)
  blocking collectives  16.9 us (3%)
  between operations  16.8 us (3%)
  other arithmetic  16 us (3%)
    psum x1, waiting for transfers between devices, body(): lax.psum(select_rows(query_up_factors), 'dp').astype(jnp.float32)  373 us
    dot_general x8, matrix products, up_group(): part_q = jnp.dot(down_q, factor_q, preferred_element_type=jnp.float32)  39.7 us
    dot_general x8, matrix products, down_group(): product = jnp.dot(tokens, factor, preferred_element_type=jnp.float32)  31.6 us
    another operation x1, loops' own time, body(): lax.fori_loop(first_req, last_req, up_group, (zero_q, zero_v))  28 us
    dot_general x1, matrix products, body(): jnp.dot(piece, query_weight, preferred_element_type=jnp.float32)  24.8 us
    psum x1, blocking collectives, body(): down = lax.psum(selected, 'tp').astype(jnp.bfloat16)  16.9 us
    gather x3, local copies, waits for them, and re-layouts, select_rows(): taken = jnp.take(table, location, axis=0)  13.3 us
  transfers between devices with their start and end apart: 2, of which 1 were waited for; matrix products, arithmetic and copies ran while one was open for 16% of the time, Pallas kernels for 0%

commit v1 on v0

--- a/solution.py
+++ b/solution.py
@@ -41,7 +41,7 @@
 
     summed = (
         lax.psum(select_rows(adapter_down_factors), "dp").astype(jnp.float32),
-        lax.psum(select_rows(query_up_factors), "dp").astype(jnp.float32),
+        jnp.sum(lax.all_gather(select_rows(query_up_factors), "dp"), axis=0).astype(jnp.float32),
         lax.psum(select_rows(value_up_factors), "dp").astype(jnp.float32),
     )
     down_f = summed[0].astype(jnp.bfloat16)

time: 587 us -> 631 us (1.075)
  waiting for transfers between devices: 373 us -> 409 us
  other arithmetic: 16 us -> 23.3 us
    all_gather x0 -> x1, waiting for transfers between devices: none -> 99.6 us  [body(): lax.all_gather(select_rows(query_up_factors), 'dp')]
    psum x1, waiting for transfers between devices: 373 us -> 299 us  [body(): lax.psum(select_rows(adapter_down_factors), 'dp').astype(jnp.float32)]
    all_gather x1, waiting for transfers between devices: 0.03 us -> 10 us  [body(): piece = lax.all_gather(tokens, 'tp', axis=1, tiled=True)]
    reduce_sum x0 -> x1, other arithmetic: none -> 7.52 us  [body(): jnp.sum(lax.all_gather(select_rows(query_up_factors), 'dp'), axis=0)]
  transfers between devices with their start and end apart: 2 -> 3, of which waited for: 1 -> 3; matrix products, arithmetic and copies ran while one was open for 16% -> 17% of each run, Pallas kernels for 0% -> 0%
where the time goes in v1:
time: 631 us; the launch traced here: 628 us
  waiting for transfers between devices  409 us (65%)
  matrix products  112 us (18%)
  loops' own time  27.9 us (4%)
  other arithmetic  23.3 us (4%)
  local copies, waits for them, and re-layouts  22.9 us (4%)
  blocking collectives  17.1 us (3%)
  between operations  15.2 us (2%)
    psum x1, waiting for transfers between devices, body(): lax.psum(select_rows(adapter_down_factors), 'dp').astype(jnp.float32)  299 us
    all_gather x1, waiting for transfers between devices, body(): lax.all_gather(select_rows(query_up_factors), 'dp')  99.6 us
    dot_general x8, matrix products, up_group(): part_q = jnp.dot(down_q, factor_q, preferred_element_type=jnp.float32)  40.6 us
    dot_general x8, matrix products, down_group(): product = jnp.dot(tokens, factor, preferred_element_type=jnp.float32)  32.6 us
    another operation x1, loops' own time, body(): lax.fori_loop(first_req, last_req, up_group, (zero_q, zero_v))  27.6 us
    dot_general x1, matrix products, body(): jnp.dot(piece, query_weight, preferred_element_type=jnp.float32)  24.8 us
    psum x1, blocking collectives, body(): down = lax.psum(selected, 'tp').astype(jnp.bfloat16)  17.1 us
  transfers between devices with their start and end apart: 3, of which 3 were waited for; matrix products, arithmetic and copies ran while one was open for 17% of the time, Pallas kernels for 0%

profile of v1, /device:TPU:20, one launch (start us, length us, event | category | flops | bytes accessed | tf_op | source)
XLA Modules:
  0.0 627.9 jit_solution(869295210236498006)
XLA Ops:
  8.0 1.3 gather_fusion
  9.4 7.3 %gather_fusion.2 = bf16[16,2048,128]{2,1,0:T(8,128)(2,1)} fusion(bf16[64,2048,128]{2,1,0:T(8,128)(2,1)} %param.16, s32[1024]{0:T(1024)S(1)} %pad_clamp_fusion), kind=kCustom, calls=%fused_computation.2 | custom fusion | bytes 16777280 | tf_op jit(solution)/shard_map/jit(_take)/gather | solution.py:39
  17.3 7.6 %select_select_fusion = bf16[16,2048,128]{2,1,0:T(8,128)(2,1)} fusion(bf16[16,2048,128]{2,1,0:T(8,128)(2,1)} %gather_fusion.2, pred[16]{0:T(512)(128)(4,1)S(1)} %get-tuple-element.124, pred[16]{0:T(512)(128)(4,1)S(1)} %get-tuple-element.123), kind=kLoop, calls=%fused_computation.22 | loop fusion | flops 8388608 | bytes 16777248 | tf_op jit(solution)/shard_map/jit(_where)/select_n | solution.py:40
  25.9 4.1 gather_fusion.1
  30.0 1.6 fusion.13
  34.7 299.1 %all-reduce.4.cloned.1.call-done = (bf16[16,2048,128]{2,1,0:T(8,128)(2,1)}, bf16[16,64,256]{2,1,0:T(8,128)(2,1)}) async-done(((bf16[16,2048,128]{2,1,0:T(8,128)(2,1)}, bf16[16,64,256]{2,1,0:T(8,128)(2,1)}), (bf16[16,2048,128]{2,1,0:T(8,128)(2,1)}, bf16[16,64,256]{2,1,0:T(8,128)(2,1)})) %all-reduce.4.cloned.1.call-update) | async-done | bytes 8912912 | tf_op jit(solution)/shard_map/psum | solution.py:43
  333.8 32.9 %while.22 = (s32[]{:T(128)}, f32[1024,128]{0,1:T(8,128)S(1)}, s32[]{:T(128)}, s32[1024]{0:T(1024)S(1)}, bf16[16,2048,128]{2,1,0:T(8,128)(2,1)}, /*index=5*/bf16[...) while((s32[]{:T(128)}, f32[1024,128]{0,1:T(8,128)S(1)}, s32[]{:T(128)}, s32[1024]{0:T(1024)S(1)}, ...), condition=%wide.region_6.7_spmd, body=%wide.region_5.6_spmd.sunk | while | flops 537134080 | bytes 5773447 | solution.py:64
  333.9 3.9 fusion.37
  337.9 4.0 fusion.37
  341.9 4.5 fusion.37
  346.4 4.3 fusion.37
  350.8 3.9 fusion.37
  354.8 4.0 fusion.37
  358.8 3.9 fusion.37
  362.8 3.9 fusion.37
  367.0 17.1 %all-reduce.5 = bf16[1024,128]{1,0:T(8,128)(2,1)S(1)} all-reduce(f32[1024,128]{1,0:T(8,128)S(1)} %copy.24), channel_id=1, replica_groups=mesh['replica'=2,'tp'=4,'dp'=4] {'tp'}, use_global_device_ids=true, to_apply=%region_7.8 | all-reduce | flops 131072 | bytes 786432 | tf_op jit(solution)/shard_map/psum | solution.py:67
  384.2 99.6 %all-gather.5.cloned.1.call-done = bf16[4,16,64,1024]{3,2,1,0:T(8,128)(2,1)} async-done(((bf16[1,16,64,1024]{3,2,1,0:T(8,128)(2,1)}), bf16[4,16,64,1024]{3,2,1,0:T(8,128)(2,1)}) %all-gather.5.cloned.1.call-update) | async-done | bytes 8388624 | tf_op jit(solution)/shard_map/all_gather | solution.py:44
  483.8 7.5 %reduce_sum.22 = bf16[16,64,1024]{2,1,0:T(8,128)(2,1)} reduce(bf16[4,16,64,1024]{3,2,1,0:T(8,128)(2,1)} %all-gather.5.cloned.1.call-done, bf16[]{:T(256)} %constant.120.clone.1), dimensions={0}, to_apply=%region_2.3 | reduce | flops 3145728 | bytes 10485762 | tf_op jit(solution)/shard_map/reduce_sum | solution.py:44
  491.3 2.7 broadcast_in_dim.118
  494.1 81.4 %while.23 = (s32[]{:T(128)}, f32[1024,1024]{0,1:T(8,128)}, f32[1024,256]{0,1:T(8,128)S(1)}, s32[]{:T(128)}, s32[1024]{0:T(1024)S(1)}, /*index=5*/bf16[16,64,1024...) while((s32[]{:T(128)}, f32[1024,1024]{0,1:T(8,128)}, ...), condition=%wide.region_9.10_spmd, body=%wide.region_8.9_spmd.sunk | while | flops 170394624 | bytes 10919075 | solution.py:82
  496.9 5.7 bitcast_add_fusion.2
  507.7 5.0 bitcast_add_fusion.2
  517.6 5.0 bitcast_add_fusion.2
  527.6 5.0 bitcast_add_fusion.2
  537.6 5.0 bitcast_add_fusion.2
  547.5 5.0 bitcast_add_fusion.2
  557.5 5.0 bitcast_add_fusion.2
  567.5 5.1 bitcast_add_fusion.2
  575.5 5.4 copy.25
  581.2 10.0 %all-gather.3.cloned.1.call-done = bf16[1024,8192]{1,0:T(8,128)(2,1)} async-done(((bf16[1024,2048]{1,0:T(8,128)(2,1)}), bf16[1024,8192]{1,0:T(8,128)(2,1)}) %all-gather.3.cloned.1.call-update) | async-done | bytes 16777232 | tf_op jit(solution)/shard_map/all_gather | solution.py:55
  591.2 24.8 %add_convert_fusion = bf16[1024,1024]{1,0:T(8,128)(2,1)} fusion(f32[1024,1024]{1,0:T(8,128)} %copy.25, bf16[1024,8192]{1,0:T(8,128)(2,1)} %all-gather.3.cloned.1.call-done, bf16[8192,1024]{1,0:T(8,128)(2,1)} %param.14), kind=kOutput, calls=%fused_computation.23 | convolution fusion | flops 17183014912 | bytes 39845888 | tf_op jit(solution)/shard_map/dot_general | solution.py:56
  616.1 5.3 fusion.14
  (60 shorter events, 18.3 us)
Async XLA Ops:
  7.2 9.6 %copy-start = (bf16[64,64,256]{2,1,0:T(8,128)(2,1)S(1)}, bf16[64,64,256]{2,1,0:T(8,128)(2,1)}, u32[]{:S(2)}) copy-start(bf16[64,64,256]{2,1,0:T(8,128)(2,1)} %param.18) | copy-start | bytes 6291460
  7.2 326.6 %all-reduce.4.cloned.1.call-start = ((), (), s32[]{:S(2)}) async-start(), calls=%async_computation.2 | async-start | bytes 17825792 | tf_op jit(solution)/shard_map/psum | solution.py:43
  25.9 457.9 %all-gather.5.cloned.1.call-start = ((), (), s32[]{:S(2)}) async-start(), calls=%async_computation.1 | async-start | bytes 10485760 | tf_op jit(solution)/shard_map/all_gather | solution.py:44
  31.6 0.8 copy-start.2
  31.6 559.6 %all-gather.3.cloned.1.call-start = ((), (), s32[]{:S(2)}) async-start(), calls=%async_computation | async-start | bytes 20971520 | tf_op jit(solution)/shard_map/all_gather | solution.py:55
  591.2 24.8 %copy-start.3 = (bf16[1024,8192]{1,0:T(8,128)(2,1)S(1)}, bf16[1024,8192]{1,0:T(8,128)(2,1)}, u32[]{:S(2)}) copy-start(bf16[1024,8192]{1,0:T(8,128)(2,1)} %all-gather.3.cloned.1.call-done) | copy-start | bytes 50331652
  591.2 24.8 %copy-start.4 = (bf16[8192,256]{1,0:T(8,128)(2,1)S(1)}, bf16[8192,256]{1,0:T(8,128)(2,1)}, u32[]{:S(2)}) copy-start(bf16[8192,256]{1,0:T(8,128)(2,1)} %param.15) | copy-start | bytes 12582916
  616.1 5.3 copy-start.1
Sparse Core Ops, SparseCore 0:
  26.0 307.7 all-reduce.3
  335.9 147.7 all-gather.4
  485.3 105.8 all-gather.2
